TPU v7x, 32 devices: a whole 2x2x4 slice. The times are simulated.
32 devices in a mesh: groups: 2 (over y), sample: 2 (over core), space: 8 (over z, x).
Axes of the slice: x: 2, y: 2, z: 4, core: 2. Of those that a mesh axis runs over, the one named last changes fastest.
Arguments:
- features: bfloat16 [4, 16, 16, 16, 128], P(('groups', 'sample'), 'space'), parts along dimension 0, may hold values from -6 to 6
- w_fine: bfloat16 [27, 128, 128], replicated, may hold values from -0.109375 to 0.109375
- w_down: bfloat16 [8, 128, 256], replicated, may hold values from -0.1875 to 0.1875
- mixing: bfloat16 [8, 8], replicated, may hold values from -2 to 2
- cotangent: bfloat16 [4, 8, 16384], P(('groups', 'sample'), None, 'space'), parts along dimension 0, may hold values from -6 to 6
Outputs:
- bottleneck: bfloat16 [4, 8, 16384], P(('groups', 'sample'), None, 'space'), parts along dimension 0
- feature_grad: bfloat16 [4, 16, 16, 16, 128], P(('groups', 'sample'), 'space'), parts along dimension 0
- fine_grad: float32 [884736], P(('groups', 'space')), parts along dimension 0
- down_grad: float32 [524288], P(('groups', 'space')), parts along dimension 0
- mixing_grad: float32 [16, 8], P(('groups', 'space')), parts along dimension 0
There are 2 independent parts, one for each index of `groups`. A program takes and returns all parts, laid end to end along the dimension named above; an argument that names none is the same for every part. Nothing has to cross between parts.
All inputs are finite; a program needn't handle non-finite values.
Results may differ from a plain program's by a relative error of at most 0.0065.
Values may be sent and summed in bfloat16 or wider, within the bound.
A program may use at most 64 MiB of HBM per device.

v0:
```python
import jax
import jax.numpy as jnp
from jax import lax
from jax.sharding import PartitionSpec as P


def with_halo(array, sides, width):
    for axis, dim in sides:
        devices, length = (lax.axis_size(axis), array.shape[dim])
        up = [(i, (i + 1) % devices) for i in range(devices - 1)]
        down = [(j, i) for i, j in up]
        last = lax.slice_in_dim(array, length - width, length, axis=dim)
        initial = lax.slice_in_dim(array, 0, width, axis=dim)
        before = lax.ppermute(last, axis, up)
        after = lax.ppermute(initial, axis, down)
        array = jnp.concatenate([before, array, after], axis=dim)
    return array


def forward_conv(padded, weight, count):
    extent_x = padded.shape[2] - 2
    extent_z = padded.shape[3] - 2
    channels = padded.shape[4]
    total = None
    for shift_y in range(3):
        for shift_x in range(3):
            pieces = [
                padded[
                    :,
                    shift_y : shift_y + count,
                    shift_x : shift_x + extent_x,
                    shift_z : shift_z + extent_z,
                    :,
                ]
                for shift_z in range(3)
            ]
            stacked = jnp.concatenate(pieces, axis=-1).reshape(-1, 3 * channels)
            first = shift_y * 9 + shift_x * 3
            kernel = weight[first : first + 3].reshape(3 * channels, weight.shape[2])
            term = jnp.dot(stacked, kernel, preferred_element_type=jnp.float32)
            total = term if total is None else total + term
    return total.reshape(padded.shape[0], count, extent_x, extent_z, weight.shape[2])


def transposed_conv(padded, weight, count):
    extent_x = padded.shape[2] - 2
    extent_z = padded.shape[3] - 2
    channels = padded.shape[4]
    total = None
    for shift_y in range(3):
        for shift_x in range(3):
            pieces = [
                padded[
                    :,
                    2 - shift_y : 2 - shift_y + count,
                    2 - shift_x : 2 - shift_x + extent_x,
                    2 - shift_z : 2 - shift_z + extent_z,
                    :,
                ]
                for shift_z in range(3)
            ]
            stacked = jnp.concatenate(pieces, axis=-1).reshape(-1, 3 * channels)
            first = shift_y * 9 + shift_x * 3
            kernel = jnp.swapaxes(weight[first : first + 3], 1, 2).reshape(
                3 * channels, weight.shape[1]
            )
            term = jnp.dot(stacked, kernel, preferred_element_type=jnp.float32)
            total = term if total is None else total + term
    return total.reshape(padded.shape[0], count, extent_x, extent_z, weight.shape[1])


def weight_terms(padded, grad, count):
    extent_x = padded.shape[2] - 2
    extent_z = padded.shape[3] - 2
    channels = padded.shape[4]
    flat_grad = grad.reshape(-1, grad.shape[4])
    blocks = []
    for shift_y in range(3):
        for shift_x in range(3):
            pieces = [
                padded[
                    :,
                    shift_y : shift_y + count,
                    shift_x : shift_x + extent_x,
                    shift_z : shift_z + extent_z,
                    :,
                ]
                for shift_z in range(3)
            ]
            stacked = jnp.concatenate(pieces, axis=-1).reshape(-1, 3 * channels)
            blocks.append(
                lax.dot_general(
                    stacked, flat_grad, (((0,), (0,)), ((), ())), preferred_element_type=jnp.float32
                )
            )
    return jnp.concatenate(blocks, axis=0).reshape(-1)


def fold_taps(hidden):
    batch, rows_here, extent_x, extent_z, channels = hidden.shape
    shaped = hidden.reshape(batch, rows_here // 2, 2, extent_x // 2, 2, extent_z // 2, 2, channels)
    return shaped.transpose(0, 1, 3, 5, 2, 4, 6, 7).reshape(-1, 8 * channels)


def unfold_taps(values, batch, rows_here, extent_x, extent_z, channels):
    shaped = values.reshape(batch, rows_here // 2, extent_x // 2, extent_z // 2, 2, 2, 2, channels)
    return shaped.transpose(0, 1, 4, 2, 5, 3, 6, 7).reshape(
        batch, rows_here, extent_x, extent_z, channels
    )


def silu_slope(value):
    sigma = jax.nn.sigmoid(value)
    return sigma * (1.0 + value * (1.0 - sigma))


def local(features, w_fine, w_down, mixing, cotangent):
    batch, rows_here, extent_x, extent_z, channels = features.shape
    coarse_ch = w_down.shape[2]
    rimmed = with_halo(features, (("space", 1),), 1)
    xpadded = jnp.pad(rimmed, ((0, 0), (0, 0), (1, 1), (1, 1), (0, 0)))
    act = forward_conv(xpadded, w_fine, rows_here)
    hidden = (features.astype(jnp.float32) + jax.nn.silu(act)).astype(jnp.bfloat16)
    folded = fold_taps(hidden)
    down_matrix = w_down.reshape(8 * channels, coarse_ch)
    coarse = jnp.dot(folded, down_matrix, preferred_element_type=jnp.float32).astype(jnp.bfloat16)
    coarse = coarse.reshape(batch, rows_here // 2, -1)
    columns = lax.all_to_all(coarse, "space", split_axis=2, concat_axis=1, tiled=True)
    mixed = jnp.stack([jnp.dot(mixing, columns[0], preferred_element_type=jnp.float32)])
    bottleneck = (columns.astype(jnp.float32) + jax.nn.silu(mixed)).astype(jnp.bfloat16)
    cot = cotangent.astype(jnp.float32)
    mixed_grad = (cot * silu_slope(mixed)).astype(jnp.bfloat16)
    term = lax.dot_general(
        mixed_grad[0], columns[0], (((1,), (1,)), ((), ())), preferred_element_type=jnp.float32
    )
    spread_list = [
        lax.dot_general(
            mixing, mixed_grad[0], (((0,), (0,)), ((), ())), preferred_element_type=jnp.float32
        )
    ]
    column_grad = (cot + jnp.stack(spread_list)).astype(jnp.bfloat16)
    coarse_grad = lax.all_to_all(column_grad, "space", split_axis=1, concat_axis=2, tiled=True)
    flat_coarse = coarse_grad.reshape(-1, coarse_ch)
    down_terms = lax.dot_general(
        folded, flat_coarse, (((0,), (0,)), ((), ())), preferred_element_type=jnp.float32
    ).reshape(-1)
    hidden_grad = unfold_taps(
        jnp.dot(flat_coarse, down_matrix.T, preferred_element_type=jnp.float32),
        batch,
        rows_here,
        extent_x,
        extent_z,
        channels,
    )
    act_grad = (hidden_grad * silu_slope(act)).astype(jnp.bfloat16)
    grad_rim = with_halo(act_grad, (("space", 1),), 1)
    gpadded = jnp.pad(grad_rim, ((0, 0), (0, 0), (1, 1), (1, 1), (0, 0)))
    spread = transposed_conv(gpadded, w_fine, rows_here)
    feature_grad = (hidden_grad + spread).astype(jnp.bfloat16)
    fine_terms = weight_terms(xpadded, act_grad, rows_here)
    scale = float(
        batch * lax.axis_size("sample") * rows_here * lax.axis_size("space") * extent_x * extent_z
    ) ** (-0.5)
    shares = (
        lax.psum_scatter(fine_terms, "space", scatter_dimension=0, tiled=True),
        lax.psum_scatter(down_terms, "space", scatter_dimension=0, tiled=True),
        lax.psum_scatter(term, "space", scatter_dimension=0, tiled=True),
    )
    totals = lax.psum((shares[0], shares[1], shares[2]), "sample")
    return (bottleneck, feature_grad, totals[0] * scale, totals[1] * scale, totals[2] * scale)


def solution(mesh):
    placed = (
        P(("groups", "sample"), "space", None, None, None),
        P(),
        P(),
        P(),
        P(("groups", "sample"), None, "space"),
    )
    return jax.shard_map(
        local,
        mesh=mesh,
        in_specs=placed,
        out_specs=(
            P(("groups", "sample"), None, "space"),
            P(("groups", "sample"), "space", None, None, None),
            P(("groups", "space")),
            P(("groups", "space")),
            P(("groups", "space"), None),
        ),
        check_vma=False,
    )
```

profile of v0, /device:TPU:0, one launch (start us, length us, event | category | flops | bytes accessed | tf_op | source)
XLA Modules:
  0.0 502.1 jit_solution(10094833240650439102)
XLA Ops:
  7.2 1.0 fusion.49
  8.1 4.9 collective-permute-start
  13.0 1.3 collective-permute-start.1
  14.3 1.5 slice_bitcast_fusion
  15.9 3.3 collective-permute-done.1
  19.4 0.4 fusion.46
  20.4 0.5 copy-done.33
  20.9 0.3 fusion.50
  21.2 0.3 convolution_add_fusion.15
  21.7 0.3 convolution_add_fusion.14
  21.9 0.3 convolution_add_fusion.13
  22.2 0.3 convolution_add_fusion.12
  22.7 0.3 convolution_add_fusion.11
  23.5 0.3 convolution_add_fusion.8
  24.1 10.2 %reshape.457 = bf16[1,1,16384]{1,0,2:T(2,128)(2,1)} reshape(bf16[64,256]{1,0:T(8,128)(2,1)S(1)} %convolution_convert_fusion) | data formatting | bytes 65536 | tf_op jit(solution)/shard_map/reshape | solution.py:127
  34.3 0.5 broadcast.164
  34.8 123.6 %reduce.5 = bf16[16384]{0:T(1024)(128)(2,1)S(1)} reduce(bf16[16384,1,1]{2,1,0:T(2,128)(2,1)} %bitcast.254, bf16[]{:T(256)} %broadcast.164), dimensions={1,2}, to_apply=%bitcast.187.reduce_sub_computation | reduce | bytes 65538
  158.4 0.6 reshape.465
  159.0 5.8 %all-to-all-start = ((bf16[8,2,1024]{2,1,0:T(2,128)(2,1)}), bf16[8,2,1024]{2,1,0:T(2,128)(2,1)S(1)}, u32[]{:S(2)}, u32[]{:S(2)}) async-start(bf16[8,2,1024]{2,1,0:T(2,128)(2,1)} %reshape.465), calls=%async_computation | async-start | bytes 65536 | tf_op jit(solution)/shard_map/all_to_all | solution.py:128
  164.8 0.6 dynamic-slice
  167.8 3.6 all-to-all-done
  171.5 10.2 %reshape.466 = bf16[16384,1,1]{2,1,0:T(2,128)(2,1)} reshape(bf16[8,2,1024]{2,1,0:T(2,128)(2,1)S(1)} %all-to-all-done) | data formatting | bytes 65536
  181.7 122.9 %bitcast_reduce_fusion = bf16[16384]{0:T(1024)(128)(2,1)S(1)} fusion(bf16[16384,1,1]{2,1,0:T(2,128)(2,1)} %reshape.466), kind=kLoop, calls=%fused_computation.128 | loop fusion | bytes 65536 | tf_op jit(solution)/shard_map/all_to_all | solution.py:128
  305.2 0.8 reduce.6
  306.1 0.6 reshape.467
  306.7 18.2 %all-reduce.4 = f32[8,8]{1,0:T(8,128)S(1)} all-reduce(f32[8,8]{1,0:T(8,128)S(1)} %fusion.39), channel_id=4, replica_groups=mesh['groups'=2,'sample'=2,'space'=8] {'space'}, use_global_device_ids=true, to_apply=%region_4.5.clone | all-reduce | flops 64 | bytes 512
  324.9 0.6 constant_dynamic-slice_fusion
  325.5 3.3 all-to-all-start.1
  328.9 2.5 psum.23
  331.4 0.6 fusion.42
  332.0 0.5 broadcast_multiply_fusion.2
  332.5 2.9 all-to-all-done.1
  335.7 0.3 multiply_convert_fusion
  336.1 0.3 fusion.10
  336.4 0.6 copy-done.4
  337.0 0.3 fusion.9
  337.3 0.6 copy-done.28
  338.0 0.3 fusion.8
  338.3 0.6 copy-done.22
  339.1 0.3 fusion.7
  339.4 0.6 copy-done.18
  340.0 0.3 fusion.6
  340.4 0.6 copy-done.12
  341.1 0.3 fusion.5
  341.4 0.6 copy-done.6
  342.1 0.3 fusion.4
  342.4 0.3 fusion.3
  342.7 0.3 fusion.2
  343.3 2.4 collective-permute-start.2
  345.7 1.5 collective-permute-start.3
  347.4 0.3 convolution_bitcast_fusion.2
  347.7 1.6 copy.90
  349.3 2.5 collective-permute-done.3
  352.1 0.4 fusion.44
  353.3 0.3 convolution_add_fusion.7
  354.2 0.3 convolution_add_fusion.4
  355.2 116.0 %all-reduce.10.cloned.1.call-done = (f32[442368]{0:T(1024)}, f32[262144]{0:T(1024)}) async-done(((f32[442368]{0:T(1024)}, f32[262144]{0:T(1024)}), (f32[442368]{0:T(1024)}, f32[262144]{0:T(1024)})) %all-reduce.10.cloned.1.call-update) | async-done | bytes 2818064
  471.3 1.6 dynamic-slice.1
  472.9 1.6 dynamic-slice.3
  474.5 0.3 convolution_add_fusion
  474.8 0.7 add_convert_fusion
  475.5 16.6 %all-reduce.12.cloned.1.call-done = (f32[55296]{0:T(1024)}, f32[32768]{0:T(1024)}) async-done(((f32[55296]{0:T(1024)}, f32[32768]{0:T(1024)}), (f32[55296]{0:T(1024)}, f32[32768]{0:T(1024)})) %all-reduce.12.cloned.1.call-update) | async-done | bytes 352272 | tf_op jit(solution)/shard_map/psum | solution.py:169
  492.1 1.6 broadcast_multiply_fusion
  493.7 1.6 broadcast_multiply_fusion.1
  (127 shorter events, 7.3 us)
Async XLA Ops:
  7.2 16.8 %copy-start = (bf16[8,128,256]{2,1,0:T(8,128)(2,1)S(1)}, bf16[8,128,256]{2,1,0:T(8,128)(2,1)}, u32[]{:S(2)}) copy-start(bf16[8,128,256]{2,1,0:T(8,128)(2,1)} %param.7) | copy-start | bytes 1572868
  7.2 12.0 %copy-start.1 = (bf16[1,2,16,16,128]{4,3,2,1,0:T(8,128)(2,1)S(1)}, bf16[1,2,16,16,128]{4,3,2,1,0:T(8,128)(2,1)}, u32[]{:S(2)}) copy-start(bf16[1,2,16,16,128]{4,3,2,1,0:T(8,128)(2,1)} %param.5) | copy-start | bytes 393220
  8.1 7.7 %collective-permute-start = (bf16[1,1,16,16,128]{4,3,2,1,0:T(8,128)(2,1)S(1)}, bf16[1,1,16,16,128]{4,3,2,1,0:T(8,128)(2,1)S(1)}, u32[]{:S(2)}, u32[]{:S(2)}) collective-permute-start(bf16[1,1,16,16,128]{4,3,2,1,0:T(8,128)(2,1)S(1)} %get-tuple-element.82), channel_id=1, source_target_pairs={{0,1},{1,2},{2,3},{3,4},{4,5},{5,6},{6,7},{8,9},{9,10},{10,11},{11... | collective-permute-start | bytes 196616 | tf_op jit(solution)/shard_map/ppermute | solution.py:14
  13.0 6.2 %collective-permute-start.1 = (bf16[1,1,16,16,128]{4,3,2,1,0:T(8,128)(2,1)S(1)}, bf16[1,1,16,16,128]{4,3,2,1,0:T(8,128)(2,1)S(1)}, u32[]{:S(2)}, u32[]{:S(2)}) collective-permute-start(bf16[1,1,16,16,128]{4,3,2,1,0:T(8,128)(2,1)S(1)} %get-tuple-element.83), channel_id=1, source_target_pairs={{1,0},{2,1},{3,2},{4,3},{5,4},{6,5},{7,6},{9,8},{10,9},{11,10},{12... | collective-permute-start | bytes 196616 | tf_op jit(solution)/shard_map/ppermute | solution.py:15
  19.7 0.6 copy-start.17
  19.8 0.7 copy-start.19
  19.8 1.7 copy-start.21
  19.8 1.7 copy-start.23
  19.8 1.7 copy-start.25
  19.8 1.7 copy-start.27
  19.8 1.7 copy-start.29
  19.8 1.7 copy-start.31
  19.8 2.7 copy-start.5
  19.8 2.7 copy-start.7
  19.9 2.7 copy-start.9
  19.9 2.7 copy-start.11
  19.9 2.7 copy-start.13
  19.9 2.7 copy-start.15
  20.0 0.9 copy-start.33
  20.0 1.2 copy-start.35
  20.4 1.5 copy-start.3
  34.8 130.0 %copy-start.39 = (u32[32]{0:T(128)S(1)}, u32[32]{0:T(128)}, u32[]{:S(2)}) copy-start(u32[32]{0:T(128)} %constant.22) | copy-start | bytes 388
  159.0 12.4 %all-to-all-start = ((bf16[8,2,1024]{2,1,0:T(2,128)(2,1)}), bf16[8,2,1024]{2,1,0:T(2,128)(2,1)S(1)}, u32[]{:S(2)}, u32[]{:S(2)}) async-start(bf16[8,2,1024]{2,1,0:T(2,128)(2,1)} %reshape.465), calls=%async_computation | async-start | bytes 65536 | tf_op jit(solution)/shard_map/all_to_all | solution.py:128
  181.7 123.0 %copy-start.37 = (bf16[1,8,2048]{2,1,0:T(8,128)(2,1)S(1)}, bf16[1,8,2048]{2,1,0:T(8,128)(2,1)}, u32[]{:S(2)}) copy-start(bf16[1,8,2048]{2,1,0:T(8,128)(2,1)} %param.9) | copy-start | bytes 98308
  181.7 123.0 %copy-start.38 = (bf16[8,8]{1,0:T(8,128)(2,1)S(1)}, bf16[8,8]{1,0:T(8,128)(2,1)}, u32[]{:S(2)}) copy-start(bf16[8,8]{1,0:T(8,128)(2,1)} %param.8) | copy-start | bytes 388
  304.6 31.5 %copy-start.34 = (bf16[1,2,16,16,128]{4,3,2,1,0:T(8,128)(2,1)S(1)}, bf16[1,2,16,16,128]{4,3,2,1,0:T(8,128)(2,1)}, u32[]{:S(2)}) copy-start(bf16[1,2,16,16,128]{4,3,2,1,0:T(8,128)(2,1)} %copy-done.33) | copy-start | bytes 393220
  304.6 31.5 %copy-start.36 = (bf16[1,2,16,16,128]{4,3,2,1,0:T(8,128)(2,1)S(1)}, bf16[1,2,16,16,128]{4,3,2,1,0:T(8,128)(2,1)}, u32[]{:S(2)}) copy-start(bf16[1,2,16,16,128]{4,3,2,1,0:T(8,128)(2,1)} %copy-done.35) | copy-start | bytes 393220
  325.5 10.0 %all-to-all-start.1 = ((bf16[8,2,1024]{2,1,0:T(2,128)(2,1)}), bf16[8,2,1024]{2,1,0:T(2,128)(2,1)S(1)}, u32[]{:S(2)}, u32[]{:S(2)}) async-start(bf16[8,2,1024]{2,1,0:T(2,128)(2,1)} %reshape.467), calls=%async_computation.1 | async-start | bytes 65536 | tf_op jit(solution)/shard_map/all_to_all | solution.py:142
  328.8 142.4 %all-reduce.10.cloned.1.call-start = ((), (), s32[]{:S(2)}) async-start(), calls=%async_computation.2 | async-start | bytes 5636096
  336.0 1.0 copy-start.4
  337.0 0.9 copy-start.28
  337.0 1.0 copy-start.30
  337.0 1.0 copy-start.32
  338.0 0.9 copy-start.22
  338.0 1.0 copy-start.24
  338.0 1.0 copy-start.26
  339.1 0.9 copy-start.18
  339.1 1.0 copy-start.20
  340.0 0.9 copy-start.12
  340.0 1.0 copy-start.14
  340.0 1.0 copy-start.16
  341.1 0.9 copy-start.6
  341.1 1.0 copy-start.8
  341.1 1.0 copy-start.10
  343.0 6.2 %copy-start.2 = (f32[3456,128]{1,0:T(8,128)}, f32[3456,128]{1,0:T(8,128)S(1)}, u32[]{:S(2)}) copy-start(f32[3456,128]{1,0:T(8,128)S(1)} %fusion.2) | copy-start | bytes 5308420
  343.3 6.0 %collective-permute-start.2 = (bf16[1,1,16,16,128]{4,3,2,1,0:T(8,128)(2,1)S(1)}, bf16[1,1,16,16,128]{4,3,2,1,0:T(8,128)(2,1)S(1)}, u32[]{:S(2)}, u32[]{:S(2)}) collective-permute-start(bf16[1,1,16,16,128]{4,3,2,1,0:T(8,128)(2,1)S(1)} %get-tuple-element.77), channel_id=1, source_target_pairs={{0,1},{1,2},{2,3},{3,4},{4,5},{5,6},{6,7},{8,9},{9,10},{10,11},{11... | collective-permute-start | bytes 196616 | tf_op jit(solution)/shard_map/ppermute | solution.py:14
  345.7 6.2 %collective-permute-start.3 = (bf16[1,1,16,16,128]{4,3,2,1,0:T(8,128)(2,1)S(1)}, bf16[1,1,16,16,128]{4,3,2,1,0:T(8,128)(2,1)S(1)}, u32[]{:S(2)}, u32[]{:S(2)}) collective-permute-start(bf16[1,1,16,16,128]{4,3,2,1,0:T(8,128)(2,1)S(1)} %get-tuple-element.78), channel_id=1, source_target_pairs={{1,0},{2,1},{3,2},{4,3},{5,4},{6,5},{7,6},{9,8},{10,9},{11,10},{12... | collective-permute-start | bytes 196616 | tf_op jit(solution)/shard_map/ppermute | solution.py:15
  349.3 142.8 %all-reduce.12.cloned.1.call-start = ((), (), s32[]{:S(2)}) async-start(), calls=%async_computation.3 | async-start | bytes 704512 | tf_op jit(solution)/shard_map/psum | solution.py:169
Sparse Core Ops, SparseCore 0:
  349.4 121.8 all-reduce.9
  474.6 17.4 all-reduce.11
where the time goes:
time: 503 us; the launch traced here: 502 us
  local copies, waits for them, and re-layouts  161 us (32%)
  waiting for transfers between devices  145 us (29%)
  other arithmetic  131 us (26%)
  blocking collectives  20.7 us (4%)
  starting transfers between devices  19.2 us (4%)
  between operations  16.2 us (3%)
  matrix products  8.79 us (2%)
    unnamed x2, other arithmetic  124 us
    all_to_all x2, local copies, waits for them, and re-layouts, local(): lax.all_to_all(coarse, 'space', split_axis=2, concat_axis=1, tiled=True)  123 us
    unnamed x3, waiting for transfers between devices  116 us
    unnamed x90, local copies, waits for them, and re-layouts  22.8 us
    unnamed x1, blocking collectives  18.2 us
    psum x1, waiting for transfers between devices, local(): totals = lax.psum((shares[0], shares[1], shares[2]), 'sample')  16.6 us
    reshape x1, local copies, waits for them, and re-layouts, local(): coarse = coarse.reshape(batch, rows_here // 2, -1)  10.2 us
  transfers between devices with their start and end apart: 8, of which 6 were waited for; matrix products, arithmetic and copies ran while one was open for 2% of the time, Pallas kernels for 0%

commit v1 on v0

--- a/solution.py
+++ b/solution.py
@@ -125,7 +125,15 @@
     down_matrix = w_down.reshape(8 * channels, coarse_ch)
     coarse = jnp.dot(folded, down_matrix, preferred_element_type=jnp.float32).astype(jnp.bfloat16)
     coarse = coarse.reshape(batch, rows_here // 2, -1)
-    columns = lax.all_to_all(coarse, "space", split_axis=2, concat_axis=1, tiled=True)
+
+    def _divide_scenes(axis_k, my_tile, at_axis, lane_axis):
+        piece_out = jnp.split(my_tile, lax.axis_size(lane_axis), axis=at_axis)
+        outcome_arr = jnp.stack(piece_out, axis=0)
+        d_next = lax.all_to_all(outcome_arr, lane_axis, 0, 0)
+        finding = jnp.concatenate(d_next, axis=axis_k)
+        return finding
+
+    columns = _divide_scenes(1, coarse, 2, "space")
     mixed = jnp.stack([jnp.dot(mixing, columns[0], preferred_element_type=jnp.float32)])
     bottleneck = (columns.astype(jnp.float32) + jax.nn.silu(mixed)).astype(jnp.bfloat16)
     cot = cotangent.astype(jnp.float32)

time: 503 us -> 237 us (0.47)
  local copies, waits for them, and re-layouts: 161 us -> 18 us
  other arithmetic: 131 us -> 8.32 us
    unnamed x2 -> x1, other arithmetic: 124 us -> 0.83 us
    all_to_all x2 -> x0, local copies, waits for them, and re-layouts: 123 us -> none  [local(): lax.all_to_all(coarse, 'space', split_axis=2, concat_axis=1, tiled=True)]
    unnamed x90 -> x96, local copies, waits for them, and re-layouts: 22.8 us -> 12.2 us
    reshape x1, local copies, waits for them, and re-layouts: 10.2 us -> 0.02 us  [local(): coarse = coarse.reshape(batch, rows_here // 2, -1)]
  transfers between devices with their start and end apart: 8 -> 8, of which waited for: 6 -> 6; matrix products, arithmetic and copies ran while one was open for 2% -> 4% of each run, Pallas kernels for 0% -> 0%
where the time goes in v1:
time: 237 us; the launch traced here: 236 us
  waiting for transfers between devices  145 us (61%)
  blocking collectives  20.7 us (9%)
  starting transfers between devices  19.2 us (8%)
  local copies, waits for them, and re-layouts  18 us (8%)
  between operations  16.3 us (7%)
  matrix products  8.8 us (4%)
  other arithmetic  8.32 us (4%)
    unnamed x3, waiting for transfers between devices  116 us
    unnamed x1, blocking collectives  18.3 us
    psum x1, waiting for transfers between devices, local(): totals = lax.psum((shares[0], shares[1], shares[2]), 'sample')  16.6 us
    unnamed x96, local copies, waits for them, and re-layouts  12.2 us
    ppermute x2, starting transfers between devices, with_halo(): before = lax.ppermute(last, axis, up)  7.26 us
    ppermute x2, waiting for transfers between devices, with_halo(): after = lax.ppermute(initial, axis, down)  5.93 us
    all_to_all x1, starting transfers between devices, _divide_scenes(): d_next = lax.all_to_all(outcome_arr, lane_axis, 0, 0)  5.75 us
  transfers between devices with their start and end apart: 8, of which 6 were waited for; matrix products, arithmetic and copies ran while one was open for 4% of the time, Pallas kernels for 0%

profile of v1, /device:TPU:0, one launch (start us, length us, event | category | flops | bytes accessed | tf_op | source)
XLA Modules:
  0.0 236.0 jit_solution(16317323931765933840)
XLA Ops:
  7.2 1.0 fusion.53
  8.1 4.9 %collective-permute-start = (bf16[1,1,16,16,128]{4,3,2,1,0:T(8,128)(2,1)S(1)}, bf16[1,1,16,16,128]{4,3,2,1,0:T(8,128)(2,1)S(1)}, u32[]{:S(2)}, u32[]{:S(2)}) collective-permute-start(bf16[1,1,16,16,128]{4,3,2,1,0:T(8,128)(2,1)S(1)} %get-tuple-element.82), channel_id=1, source_target_pairs={{0,1},{1,2},{2,3},{3,4},{4,5},{5,6},{6,7},{8,9},{9,10},{10,11},{11... | collective-permute-start | bytes 196616 | tf_op jit(solution)/shard_map/ppermute | solution.py:14
  13.0 1.3 collective-permute-start.1
  14.3 1.5 slice_bitcast_fusion.8
  15.9 3.3 %collective-permute-done.1 = bf16[1,1,16,16,128]{4,3,2,1,0:T(8,128)(2,1)S(1)} collective-permute-done((bf16[1,1,16,16,128]{4,3,2,1,0:T(8,128)(2,1)S(1)}, bf16[1,1,16,16,128]{4,3,2,1,0:T(8,128)(2,1)S(1)}, u32[]{:S(2)}, u32[]{:S(2)}) %collective-permute-start.1) | collective-permute-done | bytes 65568 | tf_op jit(solution)/shard_map/ppermute | solution.py:15
  19.4 0.4 fusion.50
  20.5 0.5 copy-done.33
  20.9 0.3 fusion.54
  21.2 0.3 convolution_add_fusion.15
  21.7 0.3 convolution_add_fusion.14
  22.0 0.3 convolution_add_fusion.13
  22.2 0.3 convolution_add_fusion.12
  22.7 0.3 convolution_add_fusion.11
  22.9 0.3 convolution_add_fusion.10
  23.2 0.3 convolution_add_fusion.9
  23.6 0.3 convolution_add_fusion.8
  24.4 0.5 broadcast.163
  24.9 0.8 reduce.3
  25.7 0.6 reshape.463
  26.4 5.8 %all-to-all-start = ((bf16[8,2,1024]{2,1,0:T(2,128)(2,1)}), bf16[8,2,1024]{2,1,0:T(2,128)(2,1)S(1)}, u32[]{:S(2)}, u32[]{:S(2)}) async-start(bf16[8,2,1024]{2,1,0:T(2,128)(2,1)} %reshape.463), calls=%async_computation | async-start | bytes 65536 | tf_op jit(solution)/shard_map/all_to_all | solution.py:132
  32.1 0.6 dynamic-slice
  35.2 3.6 %all-to-all-done = bf16[8,2,1024]{2,1,0:T(2,128)(2,1)S(1)} async-done(((bf16[8,2,1024]{2,1,0:T(2,128)(2,1)}), bf16[8,2,1024]{2,1,0:T(2,128)(2,1)S(1)}, u32[]{:S(2)}, u32[]{:S(2)}) %all-to-all-start) | async-done | bytes 32800 | tf_op jit(solution)/shard_map/all_to_all | solution.py:132
  39.4 0.8 reduce.4
  40.2 0.6 reshape.465
  40.9 18.3 %all-reduce.4 = f32[8,8]{1,0:T(8,128)S(1)} all-reduce(f32[8,8]{1,0:T(8,128)S(1)} %fusion.39), channel_id=4, replica_groups=mesh['groups'=2,'sample'=2,'space'=8] {'space'}, use_global_device_ids=true, to_apply=%region_4.5.clone | all-reduce | flops 64 | bytes 512
  59.1 0.6 constant_dynamic-slice_fusion
  59.8 3.3 %all-to-all-start.1 = ((bf16[8,2,1024]{2,1,0:T(2,128)(2,1)}), bf16[8,2,1024]{2,1,0:T(2,128)(2,1)S(1)}, u32[]{:S(2)}, u32[]{:S(2)}) async-start(bf16[8,2,1024]{2,1,0:T(2,128)(2,1)} %reshape.465), calls=%async_computation.1 | async-start | bytes 65536 | tf_op jit(solution)/shard_map/all_to_all | solution.py:150
  63.2 2.5 %psum.23 = f32[1,8]{1,0:T(1,128)S(1)} all-reduce(f32[1,8]{1,0:T(1,128)S(1)} %constant_dynamic-slice_fusion), channel_id=1, replica_groups=mesh['groups'=2,'sample'=2,'space'=8] {'sample'}, use_global_device_ids=true, to_apply=%region_5.6 | all-reduce | flops 8 | bytes 64 | tf_op jit(solution)/shard_map/psum | solution.py:177
  65.6 0.7 fusion.44
  66.3 0.5 broadcast_multiply_fusion.2
  66.8 2.9 %all-to-all-done.1 = bf16[8,2,1024]{2,1,0:T(2,128)(2,1)S(1)} async-done(((bf16[8,2,1024]{2,1,0:T(2,128)(2,1)}), bf16[8,2,1024]{2,1,0:T(2,128)(2,1)S(1)}, u32[]{:S(2)}, u32[]{:S(2)}) %all-to-all-start.1) | async-done | bytes 32800 | tf_op jit(solution)/shard_map/all_to_all | solution.py:150
  70.0 0.3 multiply_convert_fusion
  70.4 0.3 fusion.10
  70.7 0.6 copy-done.4
  71.3 0.3 fusion.9
  71.6 0.6 copy-done.28
  72.3 0.3 fusion.8
  72.6 0.6 copy-done.22
  73.3 0.3 fusion.7
  73.6 0.6 copy-done.18
  74.3 0.3 fusion.6
  74.6 0.6 copy-done.12
  75.3 0.3 fusion.5
  75.6 0.6 copy-done.6
  76.4 0.3 fusion.4
  76.7 0.3 fusion.3
  77.0 0.3 fusion.2
  77.6 2.4 %collective-permute-start.2 = (bf16[1,1,16,16,128]{4,3,2,1,0:T(8,128)(2,1)S(1)}, bf16[1,1,16,16,128]{4,3,2,1,0:T(8,128)(2,1)S(1)}, u32[]{:S(2)}, u32[]{:S(2)}) collective-permute-start(bf16[1,1,16,16,128]{4,3,2,1,0:T(8,128)(2,1)S(1)} %get-tuple-element.77), channel_id=1, source_target_pairs={{0,1},{1,2},{2,3},{3,4},{4,5},{5,6},{6,7},{8,9},{9,10},{10,11},{11... | collective-permute-start | bytes 196616 | tf_op jit(solution)/shard_map/ppermute | solution.py:14
  80.0 1.3 collective-permute-start.3
  81.4 0.3 convolution_bitcast_fusion.2
  81.8 1.5 copy.89
  83.6 2.6 %collective-permute-done.3 = bf16[1,1,16,16,128]{4,3,2,1,0:T(8,128)(2,1)S(1)} collective-permute-done((bf16[1,1,16,16,128]{4,3,2,1,0:T(8,128)(2,1)S(1)}, bf16[1,1,16,16,128]{4,3,2,1,0:T(8,128)(2,1)S(1)}, u32[]{:S(2)}, u32[]{:S(2)}) %collective-permute-start.3) | collective-permute-done | bytes 65568 | tf_op jit(solution)/shard_map/ppermute | solution.py:15
  86.3 0.4 fusion.48
  87.6 0.3 convolution_add_fusion.7
  87.9 0.3 convolution_add_fusion.6
  88.2 0.3 convolution_add_fusion.5
  88.4 0.3 convolution_add_fusion.4
  89.5 115.7 %all-reduce.10.cloned.1.call-done = (f32[442368]{0:T(1024)}, f32[262144]{0:T(1024)}) async-done(((f32[442368]{0:T(1024)}, f32[262144]{0:T(1024)}), (f32[442368]{0:T(1024)}, f32[262144]{0:T(1024)})) %all-reduce.10.cloned.1.call-update) | async-done | bytes 2818064
  205.2 1.6 dynamic-slice.1
  206.8 1.6 dynamic-slice.3
  208.7 0.7 add_convert_fusion
  209.4 16.6 %all-reduce.12.cloned.1.call-done = (f32[55296]{0:T(1024)}, f32[32768]{0:T(1024)}) async-done(((f32[55296]{0:T(1024)}, f32[32768]{0:T(1024)}), (f32[55296]{0:T(1024)}, f32[32768]{0:T(1024)})) %all-reduce.12.cloned.1.call-update) | async-done | bytes 352272 | tf_op jit(solution)/shard_map/psum | solution.py:177
  226.0 1.6 broadcast_multiply_fusion
  227.6 1.6 broadcast_multiply_fusion.1
  (133 shorter events, 6.9 us)
Async XLA Ops:
  7.2 16.8 %copy-start = (bf16[8,128,256]{2,1,0:T(8,128)(2,1)S(1)}, bf16[8,128,256]{2,1,0:T(8,128)(2,1)}, u32[]{:S(2)}) copy-start(bf16[8,128,256]{2,1,0:T(8,128)(2,1)} %param.7) | copy-start | bytes 1572868
  7.2 12.0 %copy-start.1 = (bf16[1,2,16,16,128]{4,3,2,1,0:T(8,128)(2,1)S(1)}, bf16[1,2,16,16,128]{4,3,2,1,0:T(8,128)(2,1)}, u32[]{:S(2)}) copy-start(bf16[1,2,16,16,128]{4,3,2,1,0:T(8,128)(2,1)} %param.5) | copy-start | bytes 393220
  8.1 7.7 %collective-permute-start = (bf16[1,1,16,16,128]{4,3,2,1,0:T(8,128)(2,1)S(1)}, bf16[1,1,16,16,128]{4,3,2,1,0:T(8,128)(2,1)S(1)}, u32[]{:S(2)}, u32[]{:S(2)}) collective-permute-start(bf16[1,1,16,16,128]{4,3,2,1,0:T(8,128)(2,1)S(1)} %get-tuple-element.82), channel_id=1, source_target_pairs={{0,1},{1,2},{2,3},{3,4},{4,5},{5,6},{6,7},{8,9},{9,10},{10,11},{11... | collective-permute-start | bytes 196616 | tf_op jit(solution)/shard_map/ppermute | solution.py:14
  13.0 6.2 %collective-permute-start.1 = (bf16[1,1,16,16,128]{4,3,2,1,0:T(8,128)(2,1)S(1)}, bf16[1,1,16,16,128]{4,3,2,1,0:T(8,128)(2,1)S(1)}, u32[]{:S(2)}, u32[]{:S(2)}) collective-permute-start(bf16[1,1,16,16,128]{4,3,2,1,0:T(8,128)(2,1)S(1)} %get-tuple-element.83), channel_id=1, source_target_pairs={{1,0},{2,1},{3,2},{4,3},{5,4},{6,5},{7,6},{9,8},{10,9},{11,10},{12... | collective-permute-start | bytes 196616 | tf_op jit(solution)/shard_map/ppermute | solution.py:15
  19.7 0.7 copy-start.17
  19.8 0.7 copy-start.19
  19.8 1.7 copy-start.21
  19.8 1.7 copy-start.23
  19.8 1.7 copy-start.25
  19.8 1.7 copy-start.27
  19.8 1.7 copy-start.29
  19.8 1.7 copy-start.31
  19.8 2.7 %copy-start.5 = (bf16[1,2,16,16,128]{4,3,2,1,0:T(8,128)(2,1)}, bf16[1,2,16,16,128]{4,3,2,1,0:T(8,128)(2,1)S(1)}, u32[]{:S(2)}) copy-start(bf16[1,2,16,16,128]{4,3,2,1,0:T(8,128)(2,1)S(1)} %get-tuple-element.55) | copy-start | bytes 393220
  19.8 2.7 %copy-start.7 = (bf16[1,2,16,16,128]{4,3,2,1,0:T(8,128)(2,1)}, bf16[1,2,16,16,128]{4,3,2,1,0:T(8,128)(2,1)S(1)}, u32[]{:S(2)}) copy-start(bf16[1,2,16,16,128]{4,3,2,1,0:T(8,128)(2,1)S(1)} %get-tuple-element.56) | copy-start | bytes 393220
  19.9 2.7 %copy-start.9 = (bf16[1,2,16,16,128]{4,3,2,1,0:T(8,128)(2,1)}, bf16[1,2,16,16,128]{4,3,2,1,0:T(8,128)(2,1)S(1)}, u32[]{:S(2)}) copy-start(bf16[1,2,16,16,128]{4,3,2,1,0:T(8,128)(2,1)S(1)} %get-tuple-element.57) | copy-start | bytes 393220
  19.9 2.7 %copy-start.11 = (bf16[1,2,16,16,128]{4,3,2,1,0:T(8,128)(2,1)}, bf16[1,2,16,16,128]{4,3,2,1,0:T(8,128)(2,1)S(1)}, u32[]{:S(2)}) copy-start(bf16[1,2,16,16,128]{4,3,2,1,0:T(8,128)(2,1)S(1)} %get-tuple-element.58) | copy-start | bytes 393220
  19.9 2.7 %copy-start.13 = (bf16[1,2,16,16,128]{4,3,2,1,0:T(8,128)(2,1)}, bf16[1,2,16,16,128]{4,3,2,1,0:T(8,128)(2,1)S(1)}, u32[]{:S(2)}) copy-start(bf16[1,2,16,16,128]{4,3,2,1,0:T(8,128)(2,1)S(1)} %get-tuple-element.59) | copy-start | bytes 393220
  19.9 2.7 %copy-start.15 = (bf16[1,2,16,16,128]{4,3,2,1,0:T(8,128)(2,1)}, bf16[1,2,16,16,128]{4,3,2,1,0:T(8,128)(2,1)S(1)}, u32[]{:S(2)}) copy-start(bf16[1,2,16,16,128]{4,3,2,1,0:T(8,128)(2,1)S(1)} %get-tuple-element.60) | copy-start | bytes 393220
  20.0 0.9 copy-start.33
  20.0 1.2 copy-start.35
  20.5 1.5 copy-start.3
  23.5 8.6 %copy-start.39 = (u32[32]{0:T(128)S(1)}, u32[32]{0:T(128)}, u32[]{:S(2)}) copy-start(u32[32]{0:T(128)} %constant.22) | copy-start | bytes 388
  23.9 14.9 %copy-start.37 = (bf16[1,8,2048]{2,1,0:T(8,128)(2,1)S(1)}, bf16[1,8,2048]{2,1,0:T(8,128)(2,1)}, u32[]{:S(2)}) copy-start(bf16[1,8,2048]{2,1,0:T(8,128)(2,1)} %param.9) | copy-start | bytes 98308
  23.9 14.9 %copy-start.38 = (bf16[8,8]{1,0:T(8,128)(2,1)S(1)}, bf16[8,8]{1,0:T(8,128)(2,1)}, u32[]{:S(2)}) copy-start(bf16[8,8]{1,0:T(8,128)(2,1)} %param.8) | copy-start | bytes 388
  26.4 12.4 %all-to-all-start = ((bf16[8,2,1024]{2,1,0:T(2,128)(2,1)}), bf16[8,2,1024]{2,1,0:T(2,128)(2,1)S(1)}, u32[]{:S(2)}, u32[]{:S(2)}) async-start(bf16[8,2,1024]{2,1,0:T(2,128)(2,1)} %reshape.463), calls=%async_computation | async-start | bytes 65536 | tf_op jit(solution)/shard_map/all_to_all | solution.py:132
  35.2 35.2 %copy-start.34 = (bf16[1,2,16,16,128]{4,3,2,1,0:T(8,128)(2,1)S(1)}, bf16[1,2,16,16,128]{4,3,2,1,0:T(8,128)(2,1)}, u32[]{:S(2)}) copy-start(bf16[1,2,16,16,128]{4,3,2,1,0:T(8,128)(2,1)} %copy-done.33) | copy-start | bytes 393220
  35.2 35.2 %copy-start.36 = (bf16[1,2,16,16,128]{4,3,2,1,0:T(8,128)(2,1)S(1)}, bf16[1,2,16,16,128]{4,3,2,1,0:T(8,128)(2,1)}, u32[]{:S(2)}) copy-start(bf16[1,2,16,16,128]{4,3,2,1,0:T(8,128)(2,1)} %copy-done.35) | copy-start | bytes 393220
  59.8 10.0 %all-to-all-start.1 = ((bf16[8,2,1024]{2,1,0:T(2,128)(2,1)}), bf16[8,2,1024]{2,1,0:T(2,128)(2,1)S(1)}, u32[]{:S(2)}, u32[]{:S(2)}) async-start(bf16[8,2,1024]{2,1,0:T(2,128)(2,1)} %reshape.465), calls=%async_computation.1 | async-start | bytes 65536 | tf_op jit(solution)/shard_map/all_to_all | solution.py:150
  63.1 142.1 %all-reduce.10.cloned.1.call-start = ((), (), s32[]{:S(2)}) async-start(), calls=%async_computation.2 | async-start | bytes 5636096
  70.3 1.0 copy-start.4
  71.3 0.9 copy-start.28
  71.3 1.0 copy-start.30
  71.3 1.0 copy-start.32
  72.3 0.9 copy-start.22
  72.3 1.0 copy-start.24
  72.3 1.0 copy-start.26
  73.3 0.9 copy-start.18
  73.3 1.0 copy-start.20
  74.3 0.9 copy-start.12
  74.3 1.0 copy-start.14
  74.3 1.0 copy-start.16
  75.3 0.9 copy-start.6
  75.3 1.0 copy-start.8
  75.3 1.0 copy-start.10
  77.3 6.0 %copy-start.2 = (f32[3456,128]{1,0:T(8,128)}, f32[3456,128]{1,0:T(8,128)S(1)}, u32[]{:S(2)}) copy-start(f32[3456,128]{1,0:T(8,128)S(1)} %fusion.2) | copy-start | bytes 5308420
  77.6 5.9 %collective-permute-start.2 = (bf16[1,1,16,16,128]{4,3,2,1,0:T(8,128)(2,1)S(1)}, bf16[1,1,16,16,128]{4,3,2,1,0:T(8,128)(2,1)S(1)}, u32[]{:S(2)}, u32[]{:S(2)}) collective-permute-start(bf16[1,1,16,16,128]{4,3,2,1,0:T(8,128)(2,1)S(1)} %get-tuple-element.77), channel_id=1, source_target_pairs={{0,1},{1,2},{2,3},{3,4},{4,5},{5,6},{6,7},{8,9},{9,10},{10,11},{11... | collective-permute-start | bytes 196616 | tf_op jit(solution)/shard_map/ppermute | solution.py:14
  80.0 6.2 %collective-permute-start.3 = (bf16[1,1,16,16,128]{4,3,2,1,0:T(8,128)(2,1)S(1)}, bf16[1,1,16,16,128]{4,3,2,1,0:T(8,128)(2,1)S(1)}, u32[]{:S(2)}, u32[]{:S(2)}) collective-permute-start(bf16[1,1,16,16,128]{4,3,2,1,0:T(8,128)(2,1)S(1)} %get-tuple-element.78), channel_id=1, source_target_pairs={{1,0},{2,1},{3,2},{4,3},{5,4},{6,5},{7,6},{9,8},{10,9},{11,10},{12... | collective-permute-start | bytes 196616 | tf_op jit(solution)/shard_map/ppermute | solution.py:15
  83.3 142.7 %all-reduce.12.cloned.1.call-start = ((), (), s32[]{:S(2)}) async-start(), calls=%async_computation.3 | async-start | bytes 704512 | tf_op jit(solution)/shard_map/psum | solution.py:177
Sparse Core Ops, SparseCore 0:
  83.4 121.6 all-reduce.9
  208.5 17.4 all-reduce.11
